TPU v7x, 32 devices: a whole 2x2x4 slice. The times are simulated.
32 devices in a mesh: group: 4 (over x, core), replica: 8 (over z, y).
Axes of the slice: x: 2, y: 2, z: 4, core: 2. Of those that a mesh axis runs over, the one named last changes fastest.
Arguments:
- grad_parts: bfloat16 [8, 8, 128, 512], P('replica', None, 'group'), may hold values from -1 to 1
- owner_order: int32 [8], replicated, may hold values from 0 to 7, each once
- step_count: int32 [1], replicated, may hold values from 1 to 12
- stat_old: float32 [8, 512, 512], P('replica'), as said below
- root_old: bfloat16 [8, 512, 512], P('replica'), may hold values from -0.25 to 0.25
Outputs:
- update: bfloat16 [8, 128, 512], P(None, 'group')
- stat_new: float32 [8, 512, 512], P('replica')
- root_new: bfloat16 [8, 512, 512], P('replica')
Inputs may be any that keep to these rules, and one draw needn't show every extreme that they name: `stat_old`: each matrix is symmetric positive definite.
All inputs are finite; a program needn't handle non-finite values.
Results may differ from a plain program's by a relative error of at most 0.001.
The roundings to bfloat16 on the way count: a program that leaves them out, or rounds other values in their place, can miss the bound.
Values may be sent and summed in bfloat16 or wider, within the bound.
No kernel may reach another device: no remote copies, remote signals or barrier semaphores. Data moves between devices by JAX's collectives and lax.ppermute only.
A program may use at most 64 MiB of HBM per device.

v0:
```python
import jax
import jax.numpy as jnp
from jax import lax
from jax.sharding import PartitionSpec as P

ITERS = 3
decay_rate = 0.95
epsilon = 0.001


def newton(shifted):
    identity = jnp.eye(shifted.shape[0], dtype=jnp.float32)
    frobenius = jnp.sqrt(jnp.sum(shifted * shifted))
    coupled = shifted / frobenius
    root_iter = identity * frobenius ** (-0.25)
    for repeat in range(ITERS):
        factor = (5.0 * identity - coupled) * 0.25
        root_iter = jnp.dot(root_iter, factor, precision=lax.Precision.HIGHEST)
        if repeat + 1 < ITERS:
            factor_sq = jnp.dot(factor, factor, precision=lax.Precision.HIGHEST)
            factor_quad = jnp.dot(factor_sq, factor_sq, precision=lax.Precision.HIGHEST)
            coupled = jnp.dot(factor_quad, coupled, precision=lax.Precision.HIGHEST)
    return root_iter


def local(grad_parts, owner_order, step_count, stat_old, root_old):
    local_grads = grad_parts[0]
    ordered = local_grads[owner_order]
    received = lax.all_to_all(ordered[None], "replica", split_axis=1, concat_axis=0, tiled=True)
    owned = jnp.sum(received.astype(jnp.float32), axis=0)
    partial_gram = jnp.einsum("bri,brj->bij", owned, owned, precision=lax.Precision.HIGHEST)
    products = jnp.einsum(
        "bri,bij->brj", owned.astype(jnp.bfloat16), root_old, preferred_element_type=jnp.float32
    )
    partial_norm = jnp.sum(products * products, axis=(1, 2))
    gram_matrix, update_norm = lax.psum((partial_gram, partial_norm), "group")
    grad_norm = jnp.trace(gram_matrix, axis1=1, axis2=2)
    graft_scale = jnp.sqrt(grad_norm / (update_norm + 1e-06))
    scaled = (graft_scale[:, None, None] * products).astype(jnp.bfloat16)
    gathered = lax.all_gather(scaled, "replica", axis=0, tiled=True)
    update = jnp.zeros_like(gathered).at[owner_order].set(gathered)
    stat_new = decay_rate * stat_old + (1.0 - decay_rate) * gram_matrix
    correction = 1.0 / (1.0 - decay_rate ** step_count[0].astype(jnp.float32))
    shifted = stat_new * correction + epsilon * jnp.eye(stat_new.shape[1], dtype=jnp.float32)
    root_new = lax.map(newton, shifted).astype(jnp.bfloat16)
    return (update, stat_new, root_new)


def solution(mesh):
    placed = (
        P("replica", None, "group", None),
        P(),
        P(),
        P("replica", None, None),
        P("replica", None, None),
    )
    return jax.shard_map(
        local,
        mesh=mesh,
        in_specs=placed,
        out_specs=(P(None, "group", None), P("replica", None, None), P("replica", None, None)),
        check_vma=False,
    )
```

profile of v0, /device:TPU:0, one launch (start us, length us, event | category | flops | bytes accessed | tf_op | source)
XLA Modules:
  0.0 126.4 jit_solution(15580995075982099753)
XLA Ops:
  7.2 0.0 copy-start
  7.2 0.0 all-reduce.2.cloned.1.call-start
  7.2 0.7 compare_select_fusion
  7.9 1.5 %gather_fusion = bf16[8,32,512]{2,1,0:T(8,128)(2,1)S(1)} fusion(bf16[8,32,512]{2,1,0:T(8,128)(2,1)} %bitcast.40, s32[1024]{0:T(1024)S(1)} %pad_clamp_fusion), kind=kCustom, calls=%fused_computation | custom fusion | bytes 524320 | tf_op jit(solution)/shard_map/gather | solution.py:28
  9.5 16.0 %all_to_all.4 = bf16[1,8,32,512]{3,2,0,1:T(8,128)(2,1)S(1)} all-to-all(bf16[1,8,32,512]{3,2,0,1:T(8,128)(2,1)S(1)} %bitcast.38), channel_id=1, replica_groups=mesh['group'=4,'replica'=8] {'replica'}, dimensions={1} | all-to-all | bytes 524288 | tf_op jit(solution)/shard_map/all_to_all | solution.py:29
  25.5 2.0 %convolution_bitcast_fusion = f32[1,512,512]{2,1,0:T(8,128)} fusion(f32[32,512]{1,0:T(8,128)S(1)} %convert_reduce_fusion), kind=kOutput, calls=%fused_computation.5 | convolution fusion | flops 100663296 | bytes 1114112 | tf_op jit(solution)/shard_map/bri,brj->bij/dot_general | solution.py:31
  27.5 0.0 copy-start.1
  27.5 0.0 all-reduce.2.cloned.1.call-update
  28.4 0.0 copy-done
  28.4 0.8 multiply_reduce_fusion.1
  29.2 6.3 %psum.15 = f32[1]{0:T(128)} all-reduce(f32[1]{0:T(128)} %bitcast.5), channel_id=1, replica_groups=mesh['group'=4,'replica'=8] {'group'}, use_global_device_ids=true, to_apply=%region_4.5 | all-reduce | flops 1 | bytes 8 | tf_op jit(solution)/shard_map/psum | solution.py:36
  36.1 26.8 %all-reduce.2.cloned.1.call-done = f32[1,512,512]{2,1,0:T(8,128)} async-done(((f32[1,512,512]{2,1,0:T(8,128)}), f32[1,512,512]{2,1,0:T(8,128)}) %all-reduce.2.cloned.1.call-update) | async-done | bytes 1048592 | tf_op jit(solution)/shard_map/psum | solution.py:36
  63.0 0.0 copy-done.1
  63.0 2.2 %multiply_reduce_fusion = (f32[]{:T(128)}, f32[1,512,512]{2,1,0:T(8,128)S(1)}, f32[]{:T(128)}) fusion(f32[]{:T(128)} %bitcast.8, f32[1,512,512]{2,1,0:T(8,128)} %all-reduce.2.cloned.1.call-done, f32[1,512,512]{2,1,0:T(8,128)S(1)} %copy-done.1), kind=kLoop, calls=%fused_computation.21 | loop fusion | flops 2883582 | bytes 3145740 | tf_op jit(solution)/shard_map/while/body/eval_jaxpr/reduce_sum | solution.py:13
  65.1 0.0 copy-start.2
  65.8 2.1 %fusion.6 = f32[512,512]{1,0:T(8,128)S(1)} fusion(f32[1,512,512]{2,1,0:T(8,128)S(1)} %get-tuple-element.13, f32[]{:T(128)S(6)} %sqrt.8, f32[]{:T(128)} %bitcast.8), kind=kOutput, calls=%fused_computation.12 | convolution fusion | flops 1612709888 | bytes 2097160 | tf_op jit(solution)/shard_map/while/body/eval_jaxpr/dot_general | solution.py:20
  67.9 0.0 copy-done.2
  67.9 1.8 %fusion.51 = f32[512,512]{1,0:T(8,128)S(1)} fusion(f32[512,512]{1,0:T(8,128)S(1)} %fusion.6), kind=kOutput, calls=%fused_computation.63 | convolution fusion | flops 1610612736 | bytes 2097152 | tf_op jit(solution)/shard_map/while/body/eval_jaxpr/dot_general | solution.py:21
  69.8 3.1 %fusion.8 = f32[512,512]{1,0:T(8,128)S(1)} fusion(f32[512,512]{1,0:T(8,128)S(1)} %fusion.51, f32[1,512,512]{2,1,0:T(8,128)} %copy-done.2, f32[]{:T(128)S(6)} %sqrt.8, f32[]{:T(128)} %bitcast.8), kind=kOutput, calls=%fused_computation.14 | convolution fusion | flops 1611923456 | bytes 3145736 | tf_op jit(solution)/shard_map/while/body/eval_jaxpr/dot_general | solution.py:22
  72.9 1.9 %fusion.16 = f32[512,512]{1,0:T(8,128)S(1)} fusion(f32[512,512]{1,0:T(8,128)S(1)} %fusion.8), kind=kOutput, calls=%fused_computation.28 | convolution fusion | flops 1611661312 | bytes 2097152 | tf_op jit(solution)/shard_map/while/body/eval_jaxpr/dot_general | solution.py:20
  74.9 1.8 %fusion.52 = f32[512,512]{1,0:T(8,128)S(1)} fusion(f32[512,512]{1,0:T(8,128)S(1)} %fusion.16), kind=kOutput, calls=%fused_computation.64 | convolution fusion | flops 1610612736 | bytes 2097152 | tf_op jit(solution)/shard_map/while/body/eval_jaxpr/dot_general | solution.py:21
  76.7 1.9 %fusion = f32[512,512]{1,0:T(8,128)S(1)} fusion(f32[512,512]{1,0:T(8,128)S(1)} %fusion.52, f32[512,512]{1,0:T(8,128)S(1)} %fusion.8), kind=kOutput, calls=%fused_computation.6 | convolution fusion | flops 1611661312 | bytes 3145728 | tf_op jit(solution)/shard_map/while/body/eval_jaxpr/dot_general | solution.py:22
  78.6 3.3 %fusion.3 = f32[512,512]{1,0:T(8,128)S(1)} fusion(f32[]{:T(128)S(6)} %pow.9, f32[1,512,512]{2,1,0:T(8,128)} %copy-done.2, f32[]{:T(128)S(6)} %sqrt.8, f32[]{:T(128)} %bitcast.8), kind=kOutput, calls=%fused_computation.10 | convolution fusion | flops 1613496320 | bytes 2097164 | tf_op jit(solution)/shard_map/while/body/eval_jaxpr/dot_general | solution.py:18
  82.0 1.9 %fusion.18 = f32[512,512]{1,0:T(8,128)S(1)} fusion(f32[512,512]{1,0:T(8,128)S(1)} %fusion.3, f32[512,512]{1,0:T(8,128)S(1)} %fusion.8), kind=kOutput, calls=%fused_computation.29 | convolution fusion | flops 1611661312 | bytes 3145728 | tf_op jit(solution)/shard_map/while/body/eval_jaxpr/dot_general | solution.py:18
  84.6 30.8 %all-gather = bf16[256,512]{1,0:T(8,128)(2,1)S(1)} all-gather(bf16[32,512]{1,0:T(8,128)(2,1)S(1)} %multiply_convert_fusion), channel_id=2, replica_groups=mesh['group'=4,'replica'=8] {'replica'}, dimensions={0}, use_global_device_ids=true | all-gather | bytes 294912 | tf_op jit(solution)/shard_map/all_gather | solution.py:40
  115.5 2.6 %fusion.1 = bf16[1,512,512]{2,1,0:T(8,128)(2,1)} fusion(f32[512,512]{1,0:T(8,128)S(1)} %fusion.18, f32[512,512]{1,0:T(8,128)S(1)} %fusion), kind=kOutput, calls=%fused_computation.8 | convolution fusion | flops 1610874880 | bytes 2621440 | tf_op jit(solution)/shard_map/while/body/eval_jaxpr/dot_general | solution.py:18
  118.1 0.8 scatter_fusion
  118.9 0.0 copy-start.3
  118.9 0.7 copy-done.3
  (4 shorter events, 0.1 us)
Async XLA Ops:
  7.2 21.2 %copy-start = (bf16[1,512,512]{2,1,0:T(8,128)(2,1)S(1)}, bf16[1,512,512]{2,1,0:T(8,128)(2,1)}, u32[]{:S(2)}) copy-start(bf16[1,512,512]{2,1,0:T(8,128)(2,1)} %param.9) | copy-start | bytes 1572868
  7.2 55.8 %all-reduce.2.cloned.1.call-start = ((), (), s32[]{:S(2)}) async-start(), calls=%async_computation.1 | async-start | bytes 2097152 | tf_op jit(solution)/shard_map/psum | solution.py:36
  27.5 35.4 %copy-start.1 = (f32[1,512,512]{2,1,0:T(8,128)S(1)}, f32[1,512,512]{2,1,0:T(8,128)}, u32[]{:S(2)}) copy-start(f32[1,512,512]{2,1,0:T(8,128)} %param.8) | copy-start | bytes 3145732
  65.1 2.8 %copy-start.2 = (f32[1,512,512]{2,1,0:T(8,128)}, f32[1,512,512]{2,1,0:T(8,128)S(1)}, u32[]{:S(2)}) copy-start(f32[1,512,512]{2,1,0:T(8,128)S(1)} %get-tuple-element.13) | copy-start | bytes 3145732
  118.9 0.7 copy-start.3
Sparse Core Ops, SparseCore 0:
  27.7 35.2 all-reduce.1
where the time goes:
time: 127 us; the launch traced here: 126 us
  blocking collectives  53.1 us (42%)
  waiting for transfers between devices  26.9 us (21%)
  matrix products  23.4 us (18%)
  between operations  17.1 us (13%)
  local copies, waits for them, and re-layouts  3 us (2%)
  other arithmetic  2.95 us (2%)
    all_gather x1, blocking collectives, local(): gathered = lax.all_gather(scaled, 'replica', axis=0, tiled=True)  30.8 us
    psum x1, waiting for transfers between devices, local(): gram_matrix, update_norm = lax.psum((partial_gram, partial_norm), 'group')  26.8 us
    all_to_all x1, blocking collectives, local(): lax.all_to_all(ordered[None], 'replica', split_axis=1, concat_axis=0, til...  16 us
    dot_general x3, matrix products, newton(): root_iter = jnp.dot(root_iter, factor, precision=lax.Precision.HIGHEST)  7.9 us
    psum x1, blocking collectives, local(): gram_matrix, update_norm = lax.psum((partial_gram, partial_norm), 'group')  6.27 us
    dot_general x2, matrix products, newton(): coupled = jnp.dot(factor_quad, coupled, precision=lax.Precision.HIGHEST)  5 us
    dot_general x2, matrix products, newton(): factor_sq = jnp.dot(factor, factor, precision=lax.Precision.HIGHEST)  3.98 us
    dot_general x2, matrix products, newton(): factor_quad = jnp.dot(factor_sq, factor_sq, precision=lax.Precision.HIGHEST)  3.68 us
  transfers between devices with their start and end apart: 1, of which 1 were waited for; matrix products, arithmetic and copies ran while one was open for 1% of the time, Pallas kernels for 0%

commit v1 on v0

--- a/solution.py
+++ b/solution.py
@@ -37,7 +37,8 @@
     grad_norm = jnp.trace(gram_matrix, axis1=1, axis2=2)
     graft_scale = jnp.sqrt(grad_norm / (update_norm + 1e-06))
     scaled = (graft_scale[:, None, None] * products).astype(jnp.bfloat16)
-    gathered = lax.all_gather(scaled, "replica", axis=0, tiled=True)
+    stack = jnp.stack([scaled] * lax.axis_size("replica"))
+    gathered = jnp.concatenate(lax.all_to_all(stack, "replica", 0, 0), axis=0)
     update = jnp.zeros_like(gathered).at[owner_order].set(gathered)
     stat_new = decay_rate * stat_old + (1.0 - decay_rate) * gram_matrix
     correction = 1.0 / (1.0 - decay_rate ** step_count[0].astype(jnp.float32))

time: 127 us -> 106 us (0.83)
  blocking collectives: 53.1 us -> 22.3 us
  starting transfers between devices: 0.04 us -> 5.55 us
  waiting for transfers between devices: 26.9 us -> 29.6 us
    all_gather x1 -> x0, blocking collectives: 30.8 us -> none  [local(): gathered = lax.all_gather(scaled, 'replica', axis=0, tiled=True)]
    all_to_all x0 -> x1, starting transfers between devices: none -> 5.52 us  [local(): gathered = jnp.concatenate(lax.all_to_all(stack, 'replica', 0, 0), axis=0)]
    all_to_all x0 -> x1, waiting for transfers between devices: none -> 2.71 us  [local(): gathered = jnp.concatenate(lax.all_to_all(stack, 'replica', 0, 0), axis=0)]
    dot_general x3, matrix products: 7.9 us -> 10.1 us  [newton(): root_iter = jnp.dot(root_iter, factor, precision=lax.Precision.HIGHEST)]
  transfers between devices with their start and end apart: 1 -> 2, of which waited for: 1 -> 2; matrix products, arithmetic and copies ran while one was open for 1% -> 6% of each run, Pallas kernels for 0% -> 0%
where the time goes in v1:
time: 106 us
  waiting for transfers between devices  29.6 us (28%)
  matrix products  24.3 us (23%)
  blocking collectives  22.3 us (21%)
  between operations  17.1 us (16%)
  starting transfers between devices  5.55 us (5%)
  local copies, waits for them, and re-layouts  3.72 us (4%)
  other arithmetic  2.95 us (3%)
    psum x1, waiting for transfers between devices, local(): gram_matrix, update_norm = lax.psum((partial_gram, partial_norm), 'group')  26.8 us
    all_to_all x1, blocking collectives, local(): lax.all_to_all(ordered[None], 'replica', split_axis=1, concat_axis=0, til...  16 us
    dot_general x3, matrix products, newton(): root_iter = jnp.dot(root_iter, factor, precision=lax.Precision.HIGHEST)  10.1 us
    psum x1, blocking collectives, local(): gram_matrix, update_norm = lax.psum((partial_gram, partial_norm), 'group')  6.27 us
    all_to_all x1, starting transfers between devices, local(): gathered = jnp.concatenate(lax.all_to_all(stack, 'replica', 0, 0), axis=0)  5.52 us
    dot_general x2, matrix products, newton(): factor_sq = jnp.dot(factor, factor, precision=lax.Precision.HIGHEST)  3.98 us
    dot_general x2, matrix products, newton(): coupled = jnp.dot(factor_quad, coupled, precision=lax.Precision.HIGHEST)  3.77 us
    dot_general x2, matrix products, newton(): factor_quad = jnp.dot(factor_sq, factor_sq, precision=lax.Precision.HIGHEST)  3.68 us
  transfers between devices with their start and end apart: 2, of which 2 were waited for; matrix products, arithmetic and copies ran while one was open for 6% of the time, Pallas kernels for 0%

profile of v1, /device:TPU:0, one launch (start us, length us, event | category | flops | bytes accessed | tf_op | source)
XLA Modules:
  0.0 105.5 jit_solution(12619447655755354590)
XLA Ops:
  7.2 0.0 copy-start
  7.2 0.0 all-reduce.2.cloned.1.call-start
  7.2 0.7 compare_select_fusion
  7.9 1.5 %gather_fusion = bf16[8,32,512]{2,1,0:T(8,128)(2,1)S(1)} fusion(bf16[8,32,512]{2,1,0:T(8,128)(2,1)} %bitcast.40, s32[1024]{0:T(1024)S(1)} %pad_clamp_fusion), kind=kCustom, calls=%fused_computation | custom fusion | bytes 524320 | tf_op jit(solution)/shard_map/gather | solution.py:28
  9.5 16.0 %all_to_all.14 = bf16[1,8,32,512]{3,2,0,1:T(8,128)(2,1)S(1)} all-to-all(bf16[1,8,32,512]{3,2,0,1:T(8,128)(2,1)S(1)} %bitcast.38), channel_id=1, replica_groups=mesh['group'=4,'replica'=8] {'replica'}, dimensions={1} | all-to-all | bytes 524288 | tf_op jit(solution)/shard_map/all_to_all | solution.py:29
  25.5 2.0 %convolution_bitcast_fusion = f32[1,512,512]{2,1,0:T(8,128)} fusion(f32[32,512]{1,0:T(8,128)S(1)} %convert_reduce_fusion), kind=kOutput, calls=%fused_computation.5 | convolution fusion | flops 100663296 | bytes 1114112 | tf_op jit(solution)/shard_map/bri,brj->bij/dot_general | solution.py:31
  27.5 0.0 copy-start.1
  27.5 0.0 all-reduce.2.cloned.1.call-update
  28.4 0.0 copy-done
  28.4 0.8 multiply_reduce_fusion.1
  29.2 6.3 %psum.15 = f32[1]{0:T(128)} all-reduce(f32[1]{0:T(128)} %bitcast.5), channel_id=1, replica_groups=mesh['group'=4,'replica'=8] {'group'}, use_global_device_ids=true, to_apply=%region_4.5 | all-reduce | flops 1 | bytes 8 | tf_op jit(solution)/shard_map/psum | solution.py:36
  36.1 26.8 %all-reduce.2.cloned.1.call-done = f32[1,512,512]{2,1,0:T(8,128)} async-done(((f32[1,512,512]{2,1,0:T(8,128)}), f32[1,512,512]{2,1,0:T(8,128)}) %all-reduce.2.cloned.1.call-update) | async-done | bytes 1048592 | tf_op jit(solution)/shard_map/psum | solution.py:36
  63.0 0.0 copy-done.1
  63.0 2.2 %multiply_reduce_fusion = (f32[]{:T(128)}, f32[1,512,512]{2,1,0:T(8,128)S(1)}, f32[]{:T(128)}) fusion(f32[]{:T(128)} %bitcast.8, f32[1,512,512]{2,1,0:T(8,128)} %all-reduce.2.cloned.1.call-done, f32[1,512,512]{2,1,0:T(8,128)S(1)} %copy-done.1), kind=kLoop, calls=%fused_computation.21 | loop fusion | flops 2883582 | bytes 3145740 | tf_op jit(solution)/shard_map/while/body/eval_jaxpr/reduce_sum | solution.py:13
  65.1 0.0 copy-start.2
  65.8 2.1 %fusion.6 = f32[512,512]{1,0:T(8,128)S(1)} fusion(f32[1,512,512]{2,1,0:T(8,128)S(1)} %get-tuple-element.13, f32[]{:T(128)S(6)} %sqrt.8, f32[]{:T(128)} %bitcast.8), kind=kOutput, calls=%fused_computation.12 | convolution fusion | flops 1612709888 | bytes 2097160 | tf_op jit(solution)/shard_map/while/body/eval_jaxpr/dot_general | solution.py:20
  67.9 1.8 %fusion.51 = f32[512,512]{1,0:T(8,128)S(1)} fusion(f32[512,512]{1,0:T(8,128)S(1)} %fusion.6), kind=kOutput, calls=%fused_computation.63 | convolution fusion | flops 1610612736 | bytes 2097152 | tf_op jit(solution)/shard_map/while/body/eval_jaxpr/dot_general | solution.py:21
  69.8 0.0 copy-done.2
  69.8 1.9 %fusion.8 = f32[512,512]{1,0:T(8,128)S(1)} fusion(f32[512,512]{1,0:T(8,128)S(1)} %fusion.51, f32[1,512,512]{2,1,0:T(8,128)S(1)} %get-tuple-element.13, f32[]{:T(128)S(6)} %sqrt.8, f32[]{:T(128)} %bitcast.8), kind=kOutput, calls=%fused_computation.14 | convolution fusion | flops 1611923456 | bytes 3145736 | tf_op jit(solution)/shard_map/while/body/eval_jaxpr/dot_general | solution.py:22
  71.7 1.9 %fusion.16 = f32[512,512]{1,0:T(8,128)S(1)} fusion(f32[512,512]{1,0:T(8,128)S(1)} %fusion.8), kind=kOutput, calls=%fused_computation.28 | convolution fusion | flops 1611661312 | bytes 2097152 | tf_op jit(solution)/shard_map/while/body/eval_jaxpr/dot_general | solution.py:20
  73.6 1.8 %fusion.52 = f32[512,512]{1,0:T(8,128)S(1)} fusion(f32[512,512]{1,0:T(8,128)S(1)} %fusion.16), kind=kOutput, calls=%fused_computation.64 | convolution fusion | flops 1610612736 | bytes 2097152 | tf_op jit(solution)/shard_map/while/body/eval_jaxpr/dot_general | solution.py:21
  75.5 1.8 %fusion = f32[512,512]{1,0:T(8,128)S(1)} fusion(f32[512,512]{1,0:T(8,128)S(1)} %fusion.52, f32[512,512]{1,0:T(8,128)S(1)} %fusion.8), kind=kOutput, calls=%fused_computation.6 | convolution fusion | flops 1611661312 | bytes 3145728 | tf_op jit(solution)/shard_map/while/body/eval_jaxpr/dot_general | solution.py:22
  77.4 4.3 %fusion.3 = f32[512,512]{1,0:T(8,128)} fusion(f32[]{:T(128)S(6)} %pow.9, f32[1,512,512]{2,1,0:T(8,128)} %copy-done.2, f32[]{:T(128)S(6)} %sqrt.8, f32[]{:T(128)} %bitcast.8), kind=kOutput, calls=%fused_computation.10 | convolution fusion | flops 1613496320 | bytes 2097164 | tf_op jit(solution)/shard_map/while/body/eval_jaxpr/dot_general | solution.py:18
  82.5 0.7 stack.2
  83.2 5.5 %all-to-all-start.1 = ((bf16[8,1,32,512]{3,2,1,0:T(8,128)(2,1)}), bf16[8,1,32,512]{3,2,1,0:T(8,128)(2,1)S(1)}, u32[]{:S(2)}, u32[]{:S(2)}) async-start(bf16[8,1,32,512]{3,2,1,0:T(8,128)(2,1)} %stack.2), calls=%async_computation.1 | async-start | bytes 524288 | tf_op jit(solution)/shard_map/all_to_all | solution.py:41
  88.7 3.1 %fusion.18 = f32[512,512]{1,0:T(8,128)S(1)} fusion(f32[512,512]{1,0:T(8,128)} %fusion.3, f32[512,512]{1,0:T(8,128)S(1)} %fusion.8), kind=kOutput, calls=%fused_computation.29 | convolution fusion | flops 1611661312 | bytes 3145728 | tf_op jit(solution)/shard_map/while/body/eval_jaxpr/dot_general | solution.py:18
  91.9 2.6 %fusion.1 = bf16[1,512,512]{2,1,0:T(8,128)(2,1)} fusion(f32[512,512]{1,0:T(8,128)S(1)} %fusion.18, f32[512,512]{1,0:T(8,128)S(1)} %fusion), kind=kOutput, calls=%fused_computation.8 | convolution fusion | flops 1610874880 | bytes 2621440 | tf_op jit(solution)/shard_map/while/body/eval_jaxpr/dot_general | solution.py:18
  94.5 2.7 %all-to-all-done.1 = bf16[8,1,32,512]{3,2,1,0:T(8,128)(2,1)S(1)} async-done(((bf16[8,1,32,512]{3,2,1,0:T(8,128)(2,1)}), bf16[8,1,32,512]{3,2,1,0:T(8,128)(2,1)S(1)}, u32[]{:S(2)}, u32[]{:S(2)}) %all-to-all-start.1) | async-done | bytes 262176 | tf_op jit(solution)/shard_map/all_to_all | solution.py:41
  97.2 0.8 scatter_fusion
  98.0 0.0 copy-start.3
  98.0 0.7 copy-done.3
  (4 shorter events, 0.1 us)
Async XLA Ops:
  7.2 21.2 %copy-start = (bf16[1,512,512]{2,1,0:T(8,128)(2,1)S(1)}, bf16[1,512,512]{2,1,0:T(8,128)(2,1)}, u32[]{:S(2)}) copy-start(bf16[1,512,512]{2,1,0:T(8,128)(2,1)} %param.9) | copy-start | bytes 1572868
  7.2 55.8 %all-reduce.2.cloned.1.call-start = ((), (), s32[]{:S(2)}) async-start(), calls=%async_computation.2 | async-start | bytes 2097152 | tf_op jit(solution)/shard_map/psum | solution.py:36
  27.5 35.4 %copy-start.1 = (f32[1,512,512]{2,1,0:T(8,128)S(1)}, f32[1,512,512]{2,1,0:T(8,128)}, u32[]{:S(2)}) copy-start(f32[1,512,512]{2,1,0:T(8,128)} %param.8) | copy-start | bytes 3145732
  65.1 4.6 %copy-start.2 = (f32[1,512,512]{2,1,0:T(8,128)}, f32[1,512,512]{2,1,0:T(8,128)S(1)}, u32[]{:S(2)}) copy-start(f32[1,512,512]{2,1,0:T(8,128)S(1)} %get-tuple-element.13) | copy-start | bytes 3145732
  83.2 14.0 %all-to-all-start.1 = ((bf16[8,1,32,512]{3,2,1,0:T(8,128)(2,1)}), bf16[8,1,32,512]{3,2,1,0:T(8,128)(2,1)S(1)}, u32[]{:S(2)}, u32[]{:S(2)}) async-start(bf16[8,1,32,512]{3,2,1,0:T(8,128)(2,1)} %stack.2), calls=%async_computation.1 | async-start | bytes 524288 | tf_op jit(solution)/shard_map/all_to_all | solution.py:41
  98.0 0.7 copy-start.3
Sparse Core Ops, SparseCore 0:
  27.7 35.2 all-reduce.1
